TPU v7x, 128 devices: a whole 4x4x4 slice. The times are simulated.
128 devices in a mesh: row: 8 (over z_hi, y), col: 16 (over z_lo, x, core).
Axes of the slice: x: 4, y: 4, z: 4 (z_hi: 2, z_lo: 2; z = z_hi * 2 + z_lo), core: 2. Of those that a mesh axis runs over, the one named last changes fastest.
Arguments:
- tokens: bfloat16 [2, 128, 16384], P(None, 'col', 'row'), may hold values from -6 to 6
- gate_weight: bfloat16 [16384, 26624], P(('row', 'col')), may hold values from -0.046875 to 0.046875
- up_weight: bfloat16 [16384, 26624], P(('row', 'col')), may hold values from -0.046875 to 0.046875
- down_weight: bfloat16 [16384, 26624], P(('row', 'col')), may hold values from -0.0390625 to 0.0390625
Outputs:
- block_out: bfloat16 [2, 128, 16384], P(None, 'col', 'row')
All inputs are finite; a program needn't handle non-finite values.
Results may differ from a plain program's by a relative error of at most 0.028.
Values may be sent and summed in bfloat16 or wider, within the bound.
A program may use at most 128 MiB of HBM per device.

v0:
```python
import jax
import jax.numpy as jnp
from jax import lax
from jax.sharding import Mesh
from jax.sharding import PartitionSpec as P

COL = ("col_0", "col_1", "col_2")
ROW_COL = ("row", "col_0", "col_1", "col_2")


def laid_out(tiles, dim):
    shape = list(tiles.shape[1:])
    shape[dim] *= tiles.shape[0]
    return jnp.moveaxis(tiles, 0, dim).reshape(shape)


def copy_for_each(array, axis):
    devices = lax.axis_size(axis)
    return lax.all_to_all(
        jnp.broadcast_to(array[None], (devices, *array.shape)), axis, 0, 0, tiled=True
    )


def gathered_copies(array, axis, dim):
    return laid_out(copy_for_each(array, axis), dim)


def split_up(array, dim, devices):
    shape = array.shape
    tiles = array.reshape(*shape[:dim], devices, shape[dim] // devices, *shape[dim + 1 :])
    return jnp.moveaxis(tiles, dim, 0)


def scatter_pairs(array, chips, core, dim):
    sizes = (lax.axis_size(chips), lax.axis_size(core))
    tiles = split_up(array, dim, sizes[0] * sizes[1])
    inside = tiles.shape[1:]
    tiles = tiles.reshape(*sizes, *inside).swapaxes(0, 1).reshape(-1, *inside)
    tiles = lax.psum_scatter(tiles, core, scatter_dimension=0, tiled=True)
    return lax.psum_scatter(tiles, chips, scatter_dimension=0, tiled=True)[0]


def on_device(tokens, gate_weight, up_weight, down_weight):
    batches = tokens.shape[0]

    def gate_up(batch_index, gate_tile, up_tile):
        gathered = gathered_copies(tokens[batch_index], COL, 0)
        half_width = gate_tile.shape[1]
        both_terms = jnp.concatenate(
            [
                jnp.dot(gathered, gate_tile, preferred_element_type=jnp.float32),
                jnp.dot(gathered, up_tile, preferred_element_type=jnp.float32),
            ],
            1,
        )
        summed = lax.psum(both_terms.astype(jnp.bfloat16), "row").astype(jnp.float32)
        return (jax.nn.silu(summed[:, :half_width]) * summed[:, half_width:]).astype(jnp.bfloat16)

    def project(hidden, down_tile):
        summed = scatter_pairs(
            lax.dot_general(
                hidden, down_tile, (((1,), (1,)), ((), ())), preferred_element_type=jnp.float32
            ).astype(jnp.bfloat16),
            ("col_0", "col_1"),
            "col_2",
            0,
        ).astype(jnp.float32)
        return summed.astype(jnp.bfloat16)

    gate_tile, up_tile, down_tile = (
        lax.all_to_all(gate_weight, COL, split_axis=1, concat_axis=0, tiled=True),
        lax.all_to_all(up_weight, COL, split_axis=1, concat_axis=0, tiled=True),
        lax.all_to_all(down_weight, COL, split_axis=1, concat_axis=0, tiled=True),
    )
    hiddens = [gate_up(batch_index, gate_tile, up_tile) for batch_index in range(batches)]
    outputs = [project(hidden, down_tile) for hidden in hiddens]
    return jnp.stack(outputs, 0)


def solution(mesh):
    split = Mesh(
        mesh.devices.reshape(mesh.shape["row"], 2, 4, 2), ("row", "col_0", "col_1", "col_2")
    )
    placed = (P(None, COL, "row"), P(ROW_COL, None), P(ROW_COL, None), P(ROW_COL, None))
    return jax.shard_map(
        on_device, mesh=split, in_specs=placed, out_specs=P(None, COL, "row"), check_vma=False
    )
```

profile of v0, /device:TPU:1, one launch (start us, length us, event | category | flops | bytes accessed | tf_op | source)
XLA Modules:
  0.0 487.2 jit_solution(12655868892398526695)
XLA Ops:
  7.4 16.4 %all_to_all.67 = bf16[16,8,2048]{2,1,0:T(8,128)(2,1)S(1)} all-to-all(bf16[16,8,2048]{2,1,0:T(8,128)(2,1)S(1)} %broadcast_in_dim.15), channel_id=1, replica_groups=mesh['row'=8,'col_0'=2,'col_1'=4,'col_2'=2] {'col_0','col_1','col_2'}, dimensions={0} | all-to-all | bytes 1048576 | tf_op jit(solution)/shard_map/all_to_all | solution.py:19
  23.8 0.8 broadcast_in_dim.17
  24.7 4.8 all-to-all-start.4
  29.5 9.9 %copy.9 = bf16[128,26624]{0,1:T(8,128)(2,1)} copy(bf16[128,26624]{1,0:T(8,128)(2,1)} %param.5) | data formatting | bytes 13631488 | tf_op args[1]
  40.2 5.8 %all-to-all-start.1 = ((bf16[128,16,1664]{0,2,1:T(8,128)(2,1)}), bf16[128,16,1664]{0,2,1:T(8,128)(2,1)}, u32[]{:S(2)}, u32[]{:S(2)}) async-start(bf16[128,16,1664]{0,2,1:T(8,128)(2,1)} %bitcast.46), calls=%async_computation.1 | async-start | bytes 13631488 | tf_op jit(solution)/shard_map/all_to_all | solution.py:71
  46.0 9.9 %copy.11 = bf16[128,26624]{0,1:T(8,128)(2,1)} copy(bf16[128,26624]{1,0:T(8,128)(2,1)} %param.6) | data formatting | bytes 13631488 | tf_op args[2]
  55.9 81.2 %all-to-all-done.1 = bf16[128,16,1664]{0,2,1:T(8,128)(2,1)} async-done(((bf16[128,16,1664]{0,2,1:T(8,128)(2,1)}), bf16[128,16,1664]{0,2,1:T(8,128)(2,1)}, u32[]{:S(2)}, u32[]{:S(2)}) %all-to-all-start.1) | async-done | bytes 6815776 | tf_op jit(solution)/shard_map/all_to_all | solution.py:71
  137.1 5.0 %all-to-all-start.2 = ((bf16[128,16,1664]{0,2,1:T(8,128)(2,1)}), bf16[128,16,1664]{0,2,1:T(8,128)(2,1)}, u32[]{:S(2)}, u32[]{:S(2)}) async-start(bf16[128,16,1664]{0,2,1:T(8,128)(2,1)} %bitcast.47), calls=%async_computation.2 | async-start | bytes 13631488 | tf_op jit(solution)/shard_map/all_to_all | solution.py:72
  142.1 9.8 %copy.13 = bf16[128,26624]{0,1:T(8,128)(2,1)} copy(bf16[128,26624]{1,0:T(8,128)(2,1)} %param.7) | data formatting | bytes 13631488 | tf_op args[3]
  151.9 81.1 %all-to-all-done.2 = bf16[128,16,1664]{0,2,1:T(8,128)(2,1)} async-done(((bf16[128,16,1664]{0,2,1:T(8,128)(2,1)}), bf16[128,16,1664]{0,2,1:T(8,128)(2,1)}, u32[]{:S(2)}, u32[]{:S(2)}) %all-to-all-start.2) | async-done | bytes 6815776 | tf_op jit(solution)/shard_map/all_to_all | solution.py:72
  233.0 5.1 %all-to-all-start.3 = ((bf16[128,16,1664]{0,2,1:T(8,128)(2,1)}), bf16[128,16,1664]{0,2,1:T(8,128)(2,1)}, u32[]{:S(2)}, u32[]{:S(2)}) async-start(bf16[128,16,1664]{0,2,1:T(8,128)(2,1)} %bitcast.45), calls=%async_computation.3 | async-start | bytes 13631488 | tf_op jit(solution)/shard_map/all_to_all | solution.py:73
  238.2 9.8 %copy.10 = bf16[16,128,1664]{2,1,0:T(8,128)(2,1)} copy(bf16[16,128,1664]{1,2,0:T(8,128)(2,1)} %bitcast.3) | data formatting | bytes 13631488 | tf_op jit(solution)/shard_map/all_to_all | solution.py:71
  248.0 10.0 %copy.12 = bf16[16,128,1664]{2,1,0:T(8,128)(2,1)} copy(bf16[16,128,1664]{1,2,0:T(8,128)(2,1)} %bitcast.6) | data formatting | bytes 13631488 | tf_op jit(solution)/shard_map/all_to_all | solution.py:72
  257.9 4.4 convolution_convert_fusion.2
  262.3 1.1 convolution_convert_fusion.5
  263.5 1.0 slice-done.1
  264.5 1.1 convolution_convert_fusion.1
  265.6 1.1 convolution_convert_fusion.4
  266.7 1.0 pad_maximum_fusion
  267.7 1.0 pad_maximum_fusion.1
  268.8 72.6 %all-to-all-done.3 = bf16[128,16,1664]{0,2,1:T(8,128)(2,1)} async-done(((bf16[128,16,1664]{0,2,1:T(8,128)(2,1)}), bf16[128,16,1664]{0,2,1:T(8,128)(2,1)}, u32[]{:S(2)}, u32[]{:S(2)}) %all-to-all-start.3) | async-done | bytes 6815776 | tf_op jit(solution)/shard_map/all_to_all | solution.py:73
  341.4 9.8 %copy.14 = bf16[16,128,1664]{2,1,0:T(8,128)(2,1)} copy(bf16[16,128,1664]{1,2,0:T(8,128)(2,1)} %bitcast.9) | data formatting | bytes 13631488 | tf_op jit(solution)/shard_map/all_to_all | solution.py:73
  351.1 17.9 %all-reduce.3.cloned.1.call-done = (bf16[128,3328]{1,0:T(8,128)(2,1)}, bf16[128,3328]{1,0:T(8,128)(2,1)}) async-done(((bf16[128,3328]{1,0:T(8,128)(2,1)}, bf16[128,3328]{1,0:T(8,128)(2,1)}), (bf16[128,3328]{1,0:T(8,128)(2,1)}, bf16[128,3328]{1,0:T(8,128)(2,1)})) %all-reduce.3.cloned.1.call-update) | async-done | bytes 1703952 | tf_op jit(solution)/shard_map/psum | solution.py:56
  369.0 1.3 convert_element_type.27
  370.4 5.3 %convolution_convert_fusion = bf16[128,2048]{1,0:T(8,128)(2,1)S(1)} fusion(bf16[2048,1664]{1,0:T(8,128)(2,1)} %bitcast.48, f32[128,3328]{1,0:T(8,128)S(1)} %convert_element_type.27), kind=kOutput, calls=%fused_computation | convolution fusion | flops 873955328 | bytes 9043968 | tf_op jit(solution)/shard_map/dot_general | solution.py:61
  375.6 0.8 copy.16
  376.7 5.3 %convolution_convert_fusion.3 = bf16[128,2048]{1,0:T(8,128)(2,1)S(1)} fusion(bf16[2048,1664]{1,0:T(8,128)(2,1)} %bitcast.49, f32[128,3328]{1,0:T(8,128)S(1)} %convert_element_type.24), kind=kOutput, calls=%fused_computation.3 | convolution fusion | flops 873955328 | bytes 9043968 | tf_op jit(solution)/shard_map/dot_general | solution.py:61
  382.9 8.1 %reduce-scatter.9.cloned.1.call-done = bf16[8,8,2048]{2,1,0:T(8,128)(2,1)} async-done(((bf16[16,8,2048]{2,1,0:T(8,128)(2,1)}), bf16[8,8,2048]{2,1,0:T(8,128)(2,1)}) %reduce-scatter.9.cloned.1.call-update) | async-done | bytes 262160 | tf_op jit(solution)/shard_map/reduce_scatter | solution.py:39
  391.1 14.2 %reduce-scatter.5.cloned.1.call-done = bf16[8,8,2048]{2,1,0:T(8,128)(2,1)} async-done(((bf16[16,8,2048]{2,1,0:T(8,128)(2,1)}), bf16[8,8,2048]{2,1,0:T(8,128)(2,1)}) %reduce-scatter.5.cloned.1.call-update) | async-done | bytes 262160 | tf_op jit(solution)/shard_map/reduce_scatter | solution.py:39
  405.3 35.2 %reduce-scatter.11.cloned.1.call-done = bf16[1,8,2048]{2,1,0:T(8,128)(2,1)} async-done(((bf16[8,8,2048]{2,1,0:T(8,128)(2,1)}), bf16[1,8,2048]{2,1,0:T(8,128)(2,1)}) %reduce-scatter.11.cloned.1.call-update) | async-done | bytes 32784 | tf_op jit(solution)/shard_map/reduce_scatter | solution.py:40
  440.6 38.7 %reduce-scatter.7.cloned.1.call-done = bf16[1,8,2048]{2,1,0:T(8,128)(2,1)} async-done(((bf16[8,8,2048]{2,1,0:T(8,128)(2,1)}), bf16[1,8,2048]{2,1,0:T(8,128)(2,1)}) %reduce-scatter.7.cloned.1.call-update) | async-done | bytes 32784 | tf_op jit(solution)/shard_map/reduce_scatter | solution.py:40
  479.2 1.4 pad_maximum_fusion.2
  (30 shorter events, 2.9 us)
Async XLA Ops:
  24.7 14.7 %all-to-all-start.4 = ((bf16[16,8,2048]{2,1,0:T(8,128)(2,1)}), bf16[16,8,2048]{2,1,0:T(8,128)(2,1)S(1)}, u32[]{:S(2)}, u32[]{:S(2)}) async-start(bf16[16,8,2048]{2,1,0:T(8,128)(2,1)} %broadcast_in_dim.17), calls=%async_computation.6 | async-start | bytes 1048576 | tf_op jit(solution)/shard_map/all_to_all | solution.py:19
  39.4 0.8 copy-start
  40.2 96.9 %all-to-all-start.1 = ((bf16[128,16,1664]{0,2,1:T(8,128)(2,1)}), bf16[128,16,1664]{0,2,1:T(8,128)(2,1)}, u32[]{:S(2)}, u32[]{:S(2)}) async-start(bf16[128,16,1664]{0,2,1:T(8,128)(2,1)} %bitcast.46), calls=%async_computation.1 | async-start | bytes 13631488 | tf_op jit(solution)/shard_map/all_to_all | solution.py:71
  137.1 95.9 %all-to-all-start.2 = ((bf16[128,16,1664]{0,2,1:T(8,128)(2,1)}), bf16[128,16,1664]{0,2,1:T(8,128)(2,1)}, u32[]{:S(2)}, u32[]{:S(2)}) async-start(bf16[128,16,1664]{0,2,1:T(8,128)(2,1)} %bitcast.47), calls=%async_computation.2 | async-start | bytes 13631488 | tf_op jit(solution)/shard_map/all_to_all | solution.py:72
  233.0 108.4 %all-to-all-start.3 = ((bf16[128,16,1664]{0,2,1:T(8,128)(2,1)}), bf16[128,16,1664]{0,2,1:T(8,128)(2,1)}, u32[]{:S(2)}, u32[]{:S(2)}) async-start(bf16[128,16,1664]{0,2,1:T(8,128)(2,1)} %bitcast.45), calls=%async_computation.3 | async-start | bytes 13631488 | tf_op jit(solution)/shard_map/all_to_all | solution.py:73
  238.1 130.9 %all-reduce.3.cloned.1.call-start = ((), (), s32[]{:S(2)}) async-start(), calls=%async_computation.13 | async-start | bytes 3407872 | tf_op jit(solution)/shard_map/psum | solution.py:56
  248.0 14.3 %slice-start.2 = ((s8[6815744]{0:T(1024)(128)(4,1)}), s8[2621440]{0:T(1024)(128)(4,1)S(1)}, s32[]{:S(2)}) async-start(s8[6815744]{0:T(1024)(128)(4,1)} %bitcast.42), calls=%async_computation.16 | async-start | bytes 5242880
  257.9 4.4 slice-start.3
  257.9 5.6 %slice-start = ((s8[6815744]{0:T(1024)(128)(4,1)}), s8[4194304]{0:T(1024)(128)(4,1)S(1)}, s32[]{:S(2)}) async-start(s8[6815744]{0:T(1024)(128)(4,1)} %bitcast.37), calls=%async_computation.14 | async-start | bytes 8388608
  262.3 2.1 slice-start.1
  262.3 2.1 copy-start.1
  268.7 122.2 %reduce-scatter.9.cloned.1.call-start = ((), (), s32[]{:S(2)}) async-start(), calls=%async_computation.11 | async-start | bytes 786432 | tf_op jit(solution)/shard_map/reduce_scatter | solution.py:39
  369.0 7.5 %copy-start.2 = (bf16[128,3328]{1,0:T(8,128)(2,1)S(1)}, bf16[128,3328]{1,0:T(8,128)(2,1)}, u32[]{:S(2)}) copy-start(bf16[128,3328]{1,0:T(8,128)(2,1)} %get-tuple-element.6) | copy-start | bytes 2555908
  376.5 28.8 %reduce-scatter.5.cloned.1.call-start = ((), (), s32[]{:S(2)}) async-start(), calls=%async_computation.9 | async-start | bytes 786432 | tf_op jit(solution)/shard_map/reduce_scatter | solution.py:39
  382.8 57.7 %reduce-scatter.11.cloned.1.call-start = ((), (), s32[]{:S(2)}) async-start(), calls=%async_computation.12 | async-start | bytes 294912 | tf_op jit(solution)/shard_map/reduce_scatter | solution.py:40
  391.0 88.2 %reduce-scatter.7.cloned.1.call-start = ((), (), s32[]{:S(2)}) async-start(), calls=%async_computation.10 | async-start | bytes 294912 | tf_op jit(solution)/shard_map/reduce_scatter | solution.py:40
Sparse Core Ops, SparseCore 0:
  268.9 100.1 all-reduce.2
  376.6 14.2 reduce-scatter.8
  393.3 11.9 reduce-scatter.4
  407.5 33.0 reduce-scatter.10
  442.8 36.4 reduce-scatter.6
where the time goes:
time: 494 us; the launch traced here: 487 us
  waiting for transfers between devices  349 us (71%)
  local copies, waits for them, and re-layouts  64.4 us (13%)
  starting transfers between devices  20.9 us (4%)
  matrix products  18.3 us (4%)
  blocking collectives  16.4 us (3%)
  between operations  13.3 us (3%)
    all_to_all x1, waiting for transfers between devices, on_device(): lax.all_to_all(gate_weight, COL, split_axis=1, concat_axis=0, tiled=True)  81.2 us
    all_to_all x1, waiting for transfers between devices, on_device(): lax.all_to_all(up_weight, COL, split_axis=1, concat_axis=0, tiled=True)  81.1 us
    reduce_scatter x2, waiting for transfers between devices, scatter_pairs(): return lax.psum_scatter(tiles, chips, scatter_dimension=0, tiled=True)[0]  73.9 us
    all_to_all x1, waiting for transfers between devices, on_device(): lax.all_to_all(down_weight, COL, split_axis=1, concat_axis=0, tiled=True)  72.6 us
    unnamed x17, local copies, waits for them, and re-layouts  31.5 us
    reduce_scatter x2, waiting for transfers between devices, scatter_pairs(): tiles = lax.psum_scatter(tiles, core, scatter_dimension=0, tiled=True)  22.3 us
    psum x1, waiting for transfers between devices, gate_up(): lax.psum(both_terms.astype(jnp.bfloat16), 'row').astype(jnp.float32)  17.9 us
    all_to_all x1, blocking collectives, copy_for_each(): lax.all_to_all(jnp.broadcast_to(array[None], (devices, *array.shape)), ax...  16.4 us
  transfers between devices with their start and end apart: 9, of which 8 were waited for; matrix products, arithmetic and copies ran while one was open for 15% of the time, Pallas kernels for 0%

commit v1 on v0

v1 whole, which is shorter than its diff:
```python
import jax
import jax.numpy as jnp
from jax import lax
from jax.experimental import pallas as pl
from jax.experimental.pallas import tpu as pltpu
from jax.sharding import PartitionSpec as P

MESH = pl.DeviceIdType.MESH
SIDE = 4
TILE = 128
WAVES = ((9, 9, 8),)
GATE_OF = (0, 1, 0, 1, 0, 1)
LAG = 3


class Region:
    def __init__(self, wave, color, tiles, offset):
        self.wave, self.color, self.width, self.offset = wave, color, tiles * TILE, offset
        self.axes = tuple((color + i) % 3 for i in range(3))


def regions_of(units):
    regions, offset = [], 0
    for wave, tiles in enumerate(WAVES):
        for color, count in enumerate(tiles):
            region = Region(wave, color, count, offset)
            regions.append(region)
            offset += SIDE * region.width
    assert offset == units
    return regions


def multiple(value, of):
    return pl.multiple_of(value, of)


def kernel(regions, half, *refs):
    tokens, gate_hbm, up_hbm, down_hbm, out = refs[:5]
    weights, gathered, parts, inbox, total = refs[5:10]
    (tok_send, tok_recv, tok_own, out_send, out_recv, w_own, w_send, w_recv, d_own, d_send, d_recv) = refs[10:21]
    (red_send, red_recv, all_send, all_recv) = refs[21:25]
    bufs = refs[25:]
    for index, region in enumerate(regions):
        region.index = index
        region.sums, region.box1, region.box2, region.box3, region.hidden = bufs[5 * index : 5 * index + 5]
        region.boxes = (region.box1, region.box2, region.box3)

    row, col = lax.axis_index("row"), lax.axis_index("col")
    core = lax.rem(col, 2)
    place = (
        lax.rem(lax.div(col, 2), 4),
        lax.rem(row, 4),
        lax.div(row, 4) * 2 + lax.div(col, 8),
    )
    cols = 16
    chip = lax.div(col, 2)

    def device(x, y, z):
        return (lax.div(z, 2) * 4 + y, lax.rem(z, 2) * 8 + x * 2 + core)

    def turned(value, step):
        return lax.rem(value + (step + SIDE), SIDE)

    def neighbour(axis, step):
        at = list(place)
        at[axis] = turned(at[axis], step)
        return device(*at)

    partner = (row, lax.rem(chip * 2 + 1 - core, 16))

    def peer(step):
        return lax.rem(col + step, cols)

    hbm = (gate_hbm, up_hbm, down_hbm)

    def weight_columns(region, quarter):
        if quarter is None:
            return region.offset, SIDE * region.width
        return region.offset + quarter * region.width, region.width

    def weight_copy(region, matrix, quarter, sems, remote):
        start, size = weight_columns(region, quarter)
        rows = pl.ds(multiple(core * TILE, TILE), TILE)
        here = weights.at[matrix, rows, pl.ds(multiple(start, TILE), size)]
        which = 1 - core if remote else core
        source = hbm[matrix].at[:, pl.ds(multiple(which * half + start, TILE), size)]
        own, send, recv = sems
        if not remote:
            return pltpu.make_async_copy(source, here, own)
        return pltpu.make_async_remote_copy(
            src_ref=source, dst_ref=here, send_sem=send, recv_sem=recv, device_id=partner, device_id_type=MESH
        )

    def quarters(region):
        at = place[region.axes[0]]
        return (turned(at, 2), turned(at, 1), turned(at, -1), at)

    def term_weight(region, matrix, position, remote):
        sem = position * 2 + matrix
        quarter = quarters(region)[position] if region.wave == 0 else None
        index = (region.index, sem)
        return weight_copy(region, matrix, quarter, (w_own.at[index], w_send.at[index], w_recv.at[index]), remote)

    def down_weight(region, remote):
        index = region.index
        return weight_copy(region, 2, None, (d_own.at[index], d_send.at[index], d_recv.at[index]), remote)

    def positions(region):
        return range(4) if region.wave == 0 else range(1)

    def weight_order():
        for position in range(4):
            for region in regions:
                if region.wave == 0:
                    yield region, position
        for region in regions:
            if region.wave > 0:
                yield region, 0

    def token_copy(step):
        to = peer(step)
        return pltpu.make_async_remote_copy(
            src_ref=tokens.at[:, pl.ds(multiple(lax.div(to, 2) * 256, 256), 256)],
            dst_ref=gathered.at[col],
            send_sem=tok_send.at[step],
            recv_sem=tok_recv.at[step],
            device_id=(row, to),
            device_id_type=MESH,
        )

    def token_arrival(step):
        slot = gathered.at[lax.rem(col + cols - step, cols)]
        return pltpu.make_async_remote_copy(
            src_ref=slot, dst_ref=slot, send_sem=tok_send.at[step], recv_sem=tok_recv.at[step],
            device_id=(row, peer(step)), device_id_type=MESH,
        )

    def out_copy(step):
        to = peer(step)
        return pltpu.make_async_remote_copy(
            src_ref=parts.at[to],
            dst_ref=inbox.at[col],
            send_sem=out_send.at[step],
            recv_sem=out_recv.at[step],
            device_id=(row, to),
            device_id_type=MESH,
        )

    def out_arrival(step):
        slot = inbox.at[lax.rem(col + cols - step, cols)]
        return pltpu.make_async_remote_copy(
            src_ref=slot, dst_ref=slot, send_sem=out_send.at[step], recv_sem=out_recv.at[step],
            device_id=(row, peer(step)), device_id_type=MESH,
        )

    def at_stage(region, stage):
        return place[region.axes[stage]]

    def sums_view(region, stage, matrix, quarter):
        if stage == 0:
            return region.sums.at[matrix, quarter]
        first = at_stage(region, 0)
        if stage == 1:
            return region.sums.at[matrix, first, pl.ds(multiple(quarter * 64, 64), 64)]
        start = at_stage(region, 1) * 64 + quarter * 16
        return region.sums.at[matrix, first, pl.ds(multiple(start, 16), 16)]

    def red_copy(region, stage, slot):
        step = 1 if slot < 3 else -1
        at = at_stage(region, stage)
        quarter = turned(at, 2) if slot % 3 == 0 else turned(at, step)
        index = (region.index, stage * 6 + slot)
        return pltpu.make_async_remote_copy(
            src_ref=sums_view(region, stage, GATE_OF[slot], quarter),
            dst_ref=region.boxes[stage].at[slot],
            send_sem=red_send.at[index],
            recv_sem=red_recv.at[index],
            device_id=neighbour(region.axes[stage], step),
            device_id_type=MESH,
        )

    def add_rows(target, *terms):
        rows = target.shape[0]

        @pl.loop(0, rows // 16)
        def _(block):
            at = pl.ds(multiple(block * 16, 16), 16)
            value = target[at, :].astype(jnp.float32)
            for term in terms:
                value = value + term[at, :].astype(jnp.float32)
            target[at, :] = value.astype(jnp.bfloat16)

    def terms(region, quarter):
        columns = pl.ds(multiple(region.offset + quarter * region.width, TILE), region.width)

        @pl.loop(0, 2)
        def _(matrix):
            block = gathered[...].reshape(256, 256)
            region.sums[matrix, quarter] = jnp.dot(
                block, weights[matrix, :, columns], preferred_element_type=jnp.float32
            ).astype(jnp.bfloat16)

    def wait_weights(region, position):
        for matrix in range(2):
            term_weight(region, matrix, position, False).wait()
            term_weight(region, matrix, position, True).wait_recv()

    def task_first(region):
        wait_weights(region, 0)
        terms(region, quarters(region)[0])
        red_copy(region, 0, 0).start()
        red_copy(region, 0, 3).start()

    def task_second(region):
        for position, slot in ((1, 1), (2, 4), (3, None)):
            if region.wave == 0:
                wait_weights(region, position)
            terms(region, quarters(region)[position])
            if slot is not None:
                red_copy(region, 0, slot).start()

    def task_relay(stage):
        def run(region):
            at = at_stage(region, stage)
            for slot, step in ((0, 1), (3, -1)):
                red_copy(region, stage, slot).wait_recv()
                add_rows(sums_view(region, stage, GATE_OF[slot], turned(at, step)), region.boxes[stage].at[slot])
                red_copy(region, stage, slot + 2).start()

        return run

    def arrived(region, stage):
        for slot in (1, 4, 2, 5):
            red_copy(region, stage, slot).wait_recv()

    def task_settle(stage):
        def run(region):
            at = at_stage(region, stage)
            arrived(region, stage)
            box = region.boxes[stage]
            add_rows(sums_view(region, stage, 0, at), box.at[2], box.at[4])
            add_rows(sums_view(region, stage, 1, at), box.at[1], box.at[5])
            for slot in (0, 3, 1, 4):
                red_copy(region, stage + 1, slot).start()

        return run

    def hidden_view(region, stage, quarter, part=None):
        if stage == 0:
            if part is None:
                return region.hidden.at[quarter]
            return region.hidden.at[quarter, pl.ds(part * 128, 128)]
        first = at_stage(region, 0)
        if stage == 1:
            start, size = quarter * 64, 64
            if part is not None:
                start, size = start + part * 32, 32
            return region.hidden.at[first, pl.ds(multiple(start, size), size)]
        start = at_stage(region, 1) * 64 + quarter * 16
        return region.hidden.at[first, pl.ds(multiple(start, 16), 16)]

    def forwards(region, stage):
        return (2, 3) if stage < 2 else (2 + (region.color + region.wave) % 2,)

    def all_copy(region, stage, slot, arrival=False):
        step = 1 if slot % 2 == 0 else -1
        at = at_stage(region, stage)
        if slot < 2:
            quarter, part = at, None
            landed = turned(at, -step)
        else:
            quarter, part = turned(at, -step), (slot - 2 if stage < 2 else None)
            landed = turned(at, 2)
        view = hidden_view(region, stage, landed if arrival else quarter, part)
        index = (region.index, stage * 4 + slot)
        return pltpu.make_async_remote_copy(
            src_ref=view, dst_ref=view, send_sem=all_send.at[index], recv_sem=all_recv.at[index],
            device_id=neighbour(region.axes[stage], step), device_id_type=MESH,
        )

    def task_hidden(region):
        arrived(region, 2)
        at = at_stage(region, 2)
        box = region.box3
        gate = sums_view(region, 2, 0, at)[...].astype(jnp.float32)
        gate = gate + box[2].astype(jnp.float32) + box[4].astype(jnp.float32)
        up = sums_view(region, 2, 1, at)[...].astype(jnp.float32)
        up = up + box[1].astype(jnp.float32) + box[5].astype(jnp.float32)
        hidden_view(region, 2, at)[...] = (gate / (1.0 + jnp.exp(-gate)) * up).astype(jnp.bfloat16)
        for slot in (0, 1):
            all_copy(region, 2, slot).start()

    def task_forward(stage):
        def run(region):
            for slot in (0, 1):
                all_copy(region, stage, slot, True).wait_recv()
            for slot in forwards(region, stage):
                all_copy(region, stage, slot).start()

        return run

    def task_gathered(stage):
        def run(region):
            for slot in forwards(region, stage):
                all_copy(region, stage, slot, True).wait_recv()
            for slot in (0, 1):
                all_copy(region, stage - 1, slot).start()

        return run

    def project(region, quarter):
        columns = pl.ds(multiple(region.offset + quarter * region.width, TILE), region.width)
        total[...] += lax.dot_general(
            region.hidden[quarter], weights[2, :, columns], (((1,), (1,)), ((), ())), preferred_element_type=jnp.float32
        )

    def task_project(region):
        down_weight(region, False).wait()
        down_weight(region, True).wait_recv()
        for slot in forwards(region, 0):
            all_copy(region, 0, slot, True).wait_recv()

        @pl.loop(0, SIDE)
        def _(quarter):
            project(region, quarter)

    tasks = (
        task_first, task_second, task_relay(0), task_settle(0), task_relay(1), task_settle(1), task_relay(2),
        task_hidden, task_forward(2), task_gathered(2), task_forward(1), task_gathered(1), task_forward(0), task_project,
    )

    for region, position in weight_order():
        for matrix in range(2):
            term_weight(region, matrix, position, False).start()
    own_tokens = pltpu.make_async_copy(
        tokens.at[:, pl.ds(multiple(chip * 256, 256), 256)], gathered.at[col], tok_own
    )
    own_tokens.start()

    barrier = pltpu.get_barrier_semaphore()
    for step in range(1, cols):
        pl.semaphore_signal(barrier, inc=1, device_id=(row, peer(step)), device_id_type=MESH)
    for axis in (1, 2):
        for step in (1, -1):
            pl.semaphore_signal(barrier, inc=1, device_id=neighbour(axis, step), device_id_type=MESH)
    pl.semaphore_wait(barrier, cols - 1 + 4)

    for step in range(1, cols):
        token_copy(step).start()
    for region, position in weight_order():
        for matrix in range(2):
            term_weight(region, matrix, position, True).start()
    for region in regions:
        down_weight(region, False).start()
        down_weight(region, True).start()

    total[...] = jnp.zeros_like(total)
    own_tokens.wait()
    for step in range(1, cols):
        token_arrival(step).wait_recv()

    waves = len(WAVES)
    for tick in range(len(tasks) + LAG * (waves - 1)):
        for wave in range(waves):
            number = tick - LAG * wave
            if 0 <= number < len(tasks):
                for region in regions:
                    if region.wave == wave:
                        tasks[number](region)

    parts[...] = total[...].astype(jnp.bfloat16).reshape(cols, 16, 256)
    for step in range(1, cols):
        out_copy(step).start()
    inbox[col] = parts[col]
    for step in range(1, cols):
        out_arrival(step).wait_recv()
    for block in range(cols // 2):
        out[:, block * 256 : (block + 1) * 256] = (
            inbox[2 * block].astype(jnp.float32) + inbox[2 * block + 1].astype(jnp.float32)
        ).astype(jnp.bfloat16)

    for step in range(1, cols):
        token_copy(step).wait_send()
        out_copy(step).wait_send()
    for region in regions:
        for position in positions(region):
            for matrix in range(2):
                term_weight(region, matrix, position, True).wait_send()
        down_weight(region, True).wait_send()
        for stage in range(3):
            for slot in range(6):
                red_copy(region, stage, slot).wait_send()
            for slot in (0, 1) + tuple(forwards(region, stage)):
                all_copy(region, stage, slot).wait_send()


def on_device(tokens, gate_weight, up_weight, down_weight):
    batches, block, width = tokens.shape
    units = gate_weight.shape[1]
    half = units // 2
    regions = regions_of(half)
    count = len(regions)
    bf16 = jnp.bfloat16
    dma = pltpu.SemaphoreType.DMA

    scratch = [
        pltpu.VMEM((3, 256, half), bf16),
        pltpu.VMEM((16, 16, 256), bf16),
        pltpu.VMEM((16, 16, 256), bf16),
        pltpu.VMEM((16, 16, 256), bf16),
        pltpu.VMEM((256, 256), jnp.float32),
        dma((16,)), dma((16,)), dma(()), dma((16,)), dma((16,)),
        dma((count, 8)), dma((count, 8)), dma((count, 8)),
        dma((count,)), dma((count,)), dma((count,)),
        dma((count, 18)), dma((count, 18)), dma((count, 12)), dma((count, 12)),
    ]
    for region in regions:
        w = region.width
        scratch += [
            pltpu.VMEM((2, 4, 256, w), bf16),
            pltpu.VMEM((6, 256, w), bf16),
            pltpu.VMEM((6, 64, w), bf16),
            pltpu.VMEM((6, 16, w), bf16),
            pltpu.VMEM((4, 256, w), bf16),
        ]

    anywhere = pl.BlockSpec(memory_space=pl.ANY)
    out = pl.pallas_call(
        lambda *refs: kernel(regions, half, *refs),
        out_shape=jax.ShapeDtypeStruct((batches * block, width), bf16),
        in_specs=[anywhere] * 4,
        out_specs=pl.BlockSpec(memory_space=pltpu.VMEM),
        scratch_shapes=scratch,
        name="ffn",
        compiler_params=pltpu.CompilerParams(
            collective_id=0, has_side_effects=True, vmem_limit_bytes=67_000_000
        ),
    )(tokens.reshape(batches * block, width), gate_weight, up_weight, down_weight)
    return out.reshape(batches, block, width)


def solution(mesh):
    spread = P(("row", "col"), None)
    return jax.shard_map(
        on_device,
        mesh=mesh,
        in_specs=(P(None, "col", "row"), spread, spread, spread),
        out_specs=P(None, "col", "row"),
        check_vma=False,
    )
```

time: 494 us -> 123 us (0.25); the launches traced: 487 us -> 123 us
  waiting for transfers between devices: 349 us -> 0 us
  Pallas kernels: 0 us -> 121 us
  local copies, waits for them, and re-layouts: 64.4 us -> 1.47 us
  starting transfers between devices: 20.9 us -> 0 us
  matrix products: 18.3 us -> 0 us
  blocking collectives: 16.4 us -> 0 us
  between operations: 13.3 us -> 0.01 us
    all_to_all x4 -> x0, waiting for transfers between devices: 235 us -> none  [the longest x1 81.2 us: on_device(): lax.all_to_all(gate_weight, COL, split_axis=1, concat_axis=0, tiled=True)]
    pallas_call x0 -> x1, Pallas kernels: none -> 121 us  [on_device(): pl.pallas_call(lambda *refs: kernel(regions, half, *refs), out_shape=jax....]
    reduce_scatter x4 -> x0, waiting for transfers between devices: 96.3 us -> none  [the longest x2 73.9 us: scatter_pairs(): return lax.psum_scatter(tiles, chips, scatter_dimension=0, tiled=True)[0]]
    unnamed x17 -> x1, local copies, waits for them, and re-layouts: 31.5 us -> 1.47 us
    all_to_all x3 -> x0, local copies, waits for them, and re-layouts: 29.5 us -> none  [the longest x1 9.96 us: on_device(): lax.all_to_all(up_weight, COL, split_axis=1, concat_axis=0, tiled=True)]
    all_to_all x4 -> x0, starting transfers between devices: 20.7 us -> none  [the longest x1 5.79 us: on_device(): lax.all_to_all(gate_weight, COL, split_axis=1, concat_axis=0, tiled=True)]
    dot_general x6 -> x0, matrix products: 18.3 us -> none  [the longest x2 10.5 us: project(): lax.dot_general(hidden, down_tile, (((1,), (1,)), ((), ())), preferred_el...]
    psum x1 -> x0, waiting for transfers between devices: 17.9 us -> none  [gate_up(): lax.psum(both_terms.astype(jnp.bfloat16), 'row').astype(jnp.float32)]
  transfers between devices with their start and end apart: 9 -> 0, of which waited for: 8 -> 0; matrix products, arithmetic and copies ran while one was open for 15% -> 0% of each run, Pallas kernels for 0% -> 0%
where the time goes in v1:
time: 123 us
  Pallas kernels  121 us (98%)
  local copies, waits for them, and re-layouts  1.47 us (1%)
    pallas_call x1, Pallas kernels, on_device(): pl.pallas_call(lambda *refs: kernel(regions, half, *refs), out_shape=jax....  121 us

profile of v1, /device:TPU:1, one launch (start us, length us, event | category | flops | bytes accessed | tf_op | source)
XLA Modules:
  0.0 122.8 jit_solution(10874745405150958931)
XLA Ops:
  0.0 121.3 %ffn.1 = bf16[16,2048]{1,0:T(8,128)(2,1)} custom-call(bf16[16,2048]{1,0:T(8,128)(2,1)} %bitcast.3, bf16[128,26624]{1,0:T(8,128)(2,1)} %refs_1_.1, bf16[128,26624]{1,0:T(8,128)(2,1)} %refs_2_.1, bf16[128,26624]{1,0:T(8,128)(2,1)} %refs_3_.1), custom_call_target="tpu_custom_call" | custom-call | tf_op jit(solution)/shard_map/ffn/pallas_call | solution.py:428
  121.3 1.5 %copy.6 = bf16[2,8,2048]{2,1,0:T(8,128)(2,1)} copy(bf16[2,8,2048]{2,1,0:T(8,128)(2,1)} %bitcast.2) | data formatting | bytes 131072

commit v2 on v1

v2 whole, which is shorter than its diff:
```python
import jax
import jax.numpy as jnp
from jax import lax
from jax.experimental import pallas as pl
from jax.experimental.pallas import tpu as pltpu
from jax.sharding import PartitionSpec as P

MESH = pl.DeviceIdType.MESH
SIDE = 4
TILE = 128
WAVES = ((3, 3, 3), (3, 3, 3), (3, 3, 2))
GATE_OF = (1, 0, 0, 1, 0, 1)
STEP_OF = (1, 1, -1, -1, 1, -1)
LAG = 1
ROWS = (256, 64, 16)


class Region:
    def __init__(self, wave, color, tiles, offset):
        self.wave, self.color, self.width, self.offset = wave, color, tiles * TILE, offset
        self.axes = tuple((color + i) % 3 for i in range(3))
        self.pieces = SIDE if wave == 0 else 1


def regions_of(units):
    regions, offset = [], 0
    for wave, tiles in enumerate(WAVES):
        for color, count in enumerate(tiles):
            if count == 0:
                continue
            region = Region(wave, color, count, offset)
            regions.append(region)
            offset += SIDE * region.width
    assert offset == units
    return regions


def multiple(value, of):
    return pl.multiple_of(value, of)


def kernel(regions, half, *refs):
    tokens, gate_hbm, up_hbm, down_hbm, out = refs[:5]
    weights, gathered, parts, inbox, total = refs[5:10]
    exchange, w_own, w_send, w_recv, d_own, d_send, d_recv, red_send, red_recv, all_send, all_recv = refs[10:21]
    bufs = refs[21:]
    first = 0
    for index, region in enumerate(regions):
        region.index, region.first = index, first
        first += region.pieces
        region.sums, region.box1, region.box2, region.box3, region.hidden = bufs[5 * index : 5 * index + 5]
        region.boxes = (region.box1, region.box2, region.box3)

    row, col = lax.axis_index("row"), lax.axis_index("col")
    core = lax.rem(col, 2)
    chip = lax.div(col, 2)
    place = (lax.rem(chip, 4), lax.rem(row, 4), lax.div(row, 4) * 2 + lax.div(col, 8))
    cols = 16

    def device(x, y, z):
        return (lax.div(z, 2) * 4 + y, lax.rem(z, 2) * 8 + x * 2 + core)

    around = [[lax.rem(place[axis] + step, SIDE) for step in range(SIDE)] for axis in range(3)]
    near = {}
    for axis in range(3):
        for step in (1, -1):
            at = list(place)
            at[axis] = around[axis][step]
            near[axis, step] = device(*at)
    partner = (row, chip * 2 + 1 - core)
    peers = [lax.rem(col + step, cols) for step in range(cols)]

    def drain(ref, sem):
        pltpu.make_async_copy(ref, ref, sem).wait()

    hbm = (gate_hbm, up_hbm, down_hbm)

    def weight_columns(region, quarter):
        if quarter is None:
            return region.offset, SIDE * region.width
        return region.offset + quarter * region.width, region.width

    def weight_copy(region, matrix, quarter, sems, remote):
        start, size = weight_columns(region, quarter)
        rows = pl.ds(multiple(core * TILE, TILE), TILE)
        here = weights.at[matrix, rows, pl.ds(multiple(start, TILE), size)]
        which = 1 - core if remote else core
        source = hbm[matrix].at[:, pl.ds(multiple(which * half + start, TILE), size)]
        own, send, recv = sems
        if not remote:
            return pltpu.make_async_copy(source, here, own)
        return pltpu.make_async_remote_copy(
            src_ref=source, dst_ref=here, send_sem=send, recv_sem=recv, device_id=partner, device_id_type=MESH
        )

    def quarters(region):
        return [around[region.axes[0]][step] for step in (2, 1, -1, 0)]

    def term_weight(region, matrix, position, remote):
        quarter = quarters(region)[position] if region.wave == 0 else None
        index = region.first + position
        sems = (w_own.at[index], w_send.at[region.index], w_recv.at[index])
        return weight_copy(region, matrix, quarter, sems, remote)

    def wait_weights(region, position):
        start, size = weight_columns(region, quarters(region)[position] if region.wave == 0 else None)
        both = weights.at[pl.ds(0, 2), pl.ds(0, TILE), pl.ds(multiple(start, TILE), size)]
        drain(both, w_own.at[region.first + position])
        drain(both, w_recv.at[region.first + position])

    def down_weight(region, remote):
        index = region.index
        return weight_copy(region, 2, None, (d_own.at[index], d_send.at[index], d_recv.at[index]), remote)

    def weight_order():
        for position in range(4):
            for region in regions:
                if region.wave == 0:
                    yield region, position
        for region in regions:
            if region.wave > 0:
                yield region, 0

    def token_copy(step):
        to = peers[step]
        return pltpu.make_async_remote_copy(
            src_ref=tokens.at[:, pl.ds(multiple(lax.div(to, 2) * 256, 256), 256)],
            dst_ref=gathered.at[col],
            send_sem=exchange.at[0],
            recv_sem=exchange.at[1],
            device_id=(row, to),
            device_id_type=MESH,
        )

    def out_copy(step):
        to = peers[step]
        return pltpu.make_async_remote_copy(
            src_ref=parts.at[to],
            dst_ref=inbox.at[col],
            send_sem=exchange.at[2],
            recv_sem=exchange.at[3],
            device_id=(row, to),
            device_id_type=MESH,
        )

    others = pl.ds(0, cols - 1)

    def at_stage(region, stage, step=0):
        return around[region.axes[stage]][step]

    def rows_from(region, stage, step):
        if stage == 1:
            return multiple(at_stage(region, 1, step) * 64, 64)
        return multiple(at_stage(region, 1) * 64 + at_stage(region, 2, step) * 16, 16)

    def sums_view(region, stage, matrix, step):
        if stage == 0:
            return region.sums.at[matrix, at_stage(region, 0, step)]
        return region.sums.at[matrix, at_stage(region, 0), pl.ds(rows_from(region, stage, step), ROWS[stage])]

    def send_sums(region, stage, *slots):
        for slot in slots:
            step = STEP_OF[slot]
            pltpu.make_async_remote_copy(
                src_ref=sums_view(region, stage, GATE_OF[slot], step if slot < 4 else 2),
                dst_ref=region.boxes[stage].at[slot],
                send_sem=red_send.at[region.index * 3 + stage],
                recv_sem=red_recv.at[(region.index * 3 + stage) * 3 + max(slot - 3, 0)],
                device_id=near[region.axes[stage], step],
                device_id_type=MESH,
            ).start()

    def arrived(region, stage, group):
        box = region.boxes[stage]
        drain(box.at[pl.ds(0, 4)] if group == 0 else box.at[group + 3], red_recv.at[(region.index * 3 + stage) * 3 + group])

    def add_rows(target, *terms):
        count = target.shape[0] // 16
        together = min(count, 4)

        @pl.loop(0, count // together)
        def _(outer):
            for inner in range(together):
                at = pl.ds(multiple((outer * together + inner) * 16, 16), 16)
                value = target[at, :]
                for term in terms:
                    value = value + term[at, :]
                target[at, :] = value

    def terms(region, quarter):
        columns = pl.ds(multiple(region.offset + quarter * region.width, TILE), region.width)

        block = gathered[...].reshape(256, 256)
        for matrix in range(2):
            region.sums[matrix, quarter] = jnp.dot(
                block, weights[matrix, :, columns], preferred_element_type=jnp.float32
            ).astype(jnp.bfloat16)

    def task_first(region):
        wait_weights(region, 0)
        terms(region, quarters(region)[0])
        send_sums(region, 0, 4, 5)

    def task_second(region):
        for position, slot in ((1, 0), (2, 2), (3, None)):
            if region.wave == 0:
                wait_weights(region, position)
            terms(region, quarters(region)[position])
            if slot is not None:
                send_sums(region, 0, slot)

    def task_relay(stage):
        def run(region):
            for group, step, slot in ((1, 1, 1), (2, -1, 3)):
                arrived(region, stage, group)
                add_rows(sums_view(region, stage, group - 1, step), region.boxes[stage].at[group + 3])
                send_sums(region, stage, slot)

        return run

    def task_settle(stage):
        def run(region):
            arrived(region, stage, 0)
            box = region.boxes[stage]
            add_rows(sums_view(region, stage, 0, 0), box.at[1], box.at[2])
            add_rows(sums_view(region, stage, 1, 0), box.at[0], box.at[3])
            send_sums(region, stage + 1, 4, 5, 0, 2)

        return run

    def hidden_view(region, stage, step, part=None):
        size = ROWS[stage]
        if stage == 0:
            at, start = at_stage(region, 0, step), 0
            if part is None:
                return region.hidden.at[at]
        else:
            at, start = at_stage(region, 0), rows_from(region, stage, step)
        if part is not None:
            size //= 2
            start = start + part * size
        return region.hidden.at[at, pl.ds(start if isinstance(start, int) else multiple(start, 16), size)]

    def forwards(region, stage):
        return (2, 3) if stage < 2 else (2 + (region.color + region.wave) % 2,)

    def send_hidden(region, stage, *slots):
        for slot in slots:
            step = 1 if slot % 2 == 0 else -1
            view = hidden_view(region, stage, 0 if slot < 2 else -step, slot - 2 if slot >= 2 and stage < 2 else None)
            pltpu.make_async_remote_copy(
                src_ref=view,
                dst_ref=view,
                send_sem=all_send.at[region.index * 3 + stage],
                recv_sem=all_recv.at[(region.index * 3 + stage) * 2 + slot // 2],
                device_id=near[region.axes[stage], step],
                device_id_type=MESH,
            ).start()

    def hidden_rows(region, stage, count):
        if stage == 0 and count > 1:
            return region.hidden.at[pl.ds(0, count)]
        return region.hidden.at[0, pl.ds(0, ROWS[stage] * count)]

    def reached(region, stage, group):
        drain(hidden_rows(region, stage, 2 - group), all_recv.at[(region.index * 3 + stage) * 2 + group])

    def task_hidden(region):
        arrived(region, 2, 0)
        box = region.box3
        gate = sums_view(region, 2, 0, 0)[...].astype(jnp.float32)
        gate = gate + box[1].astype(jnp.float32) + box[2].astype(jnp.float32)
        up = sums_view(region, 2, 1, 0)[...].astype(jnp.float32)
        up = up + box[0].astype(jnp.float32) + box[3].astype(jnp.float32)
        hidden_view(region, 2, 0)[...] = (gate / (1.0 + jnp.exp(-gate)) * up).astype(jnp.bfloat16)
        send_hidden(region, 2, 0, 1)

    def task_forward(stage):
        def run(region):
            reached(region, stage, 0)
            send_hidden(region, stage, *forwards(region, stage))

        return run

    def task_gathered(stage):
        def run(region):
            reached(region, stage, 1)
            send_hidden(region, stage - 1, 0, 1)

        return run

    def project(region, quarter):
        columns = pl.ds(multiple(region.offset + quarter * region.width, TILE), region.width)
        total[...] += lax.dot_general(
            region.hidden[quarter], weights[2, :, columns], (((1,), (1,)), ((), ())), preferred_element_type=jnp.float32
        )

    def task_project(region):
        drain(weights.at[2, pl.ds(0, TILE), pl.ds(region.offset, SIDE * region.width)], d_own.at[region.index])
        drain(weights.at[2, pl.ds(0, TILE), pl.ds(region.offset, SIDE * region.width)], d_recv.at[region.index])
        reached(region, 0, 1)

        for quarter in range(SIDE):
            project(region, quarter)

    tasks = (
        task_first, task_second, task_relay(0), task_settle(0), task_relay(1), task_settle(1), task_relay(2),
        task_hidden, task_forward(2), task_gathered(2), task_forward(1), task_gathered(1), task_forward(0), task_project,
    )

    for region, position in weight_order():
        for matrix in range(2):
            term_weight(region, matrix, position, False).start()
    own_tokens = pltpu.make_async_copy(
        tokens.at[:, pl.ds(multiple(chip * 256, 256), 256)], gathered.at[col], exchange.at[4]
    )
    own_tokens.start()

    barrier = pltpu.get_barrier_semaphore()
    for step in range(1, cols):
        pl.semaphore_signal(barrier, inc=1, device_id=(row, peers[step]), device_id_type=MESH)
    for axis in (1, 2):
        for step in (1, -1):
            pl.semaphore_signal(barrier, inc=1, device_id=near[axis, step], device_id_type=MESH)
    pl.semaphore_wait(barrier, cols - 1 + 4)

    for step in range(1, cols):
        token_copy(step).start()
    for region, position in weight_order():
        for matrix in range(2):
            term_weight(region, matrix, position, True).start()
    for region in regions:
        down_weight(region, False).start()
        down_weight(region, True).start()

    total[...] = jnp.zeros_like(total)
    own_tokens.wait()
    drain(gathered.at[others], exchange.at[1])

    waves = len(WAVES)
    for tick in range(len(tasks) + LAG * (waves - 1)):
        for wave in range(waves):
            number = tick - LAG * wave
            if 0 <= number < len(tasks):
                for region in regions:
                    if region.wave == wave:
                        tasks[number](region)

    parts[...] = total[...].astype(jnp.bfloat16).reshape(cols, 16, 256)
    for step in range(1, cols):
        out_copy(step).start()
    inbox[col] = parts[col]
    drain(inbox.at[others], exchange.at[3])
    for block in range(cols // 2):
        out[:, block * 256 : (block + 1) * 256] = (
            inbox[2 * block].astype(jnp.float32) + inbox[2 * block + 1].astype(jnp.float32)
        ).astype(jnp.bfloat16)

    drain(gathered.at[others], exchange.at[0])
    drain(parts.at[others], exchange.at[2])
    for region in regions:
        columns = pl.ds(region.offset, SIDE * region.width)
        drain(weights.at[pl.ds(0, 2), pl.ds(0, TILE), columns], w_send.at[region.index])
        drain(weights.at[2, pl.ds(0, TILE), columns], d_send.at[region.index])
        for stage in range(3):
            drain(region.boxes[stage], red_send.at[region.index * 3 + stage])
            drain(hidden_rows(region, stage, 3), all_send.at[region.index * 3 + stage])


def on_device(tokens, gate_weight, up_weight, down_weight):
    batches, block, width = tokens.shape
    units = gate_weight.shape[1]
    half = units // 2
    regions = regions_of(half)
    count = len(regions)
    pieces = sum(region.pieces for region in regions)
    bf16 = jnp.bfloat16
    dma = pltpu.SemaphoreType.DMA

    scratch = [
        pltpu.VMEM((3, 256, half), bf16),
        pltpu.VMEM((16, 16, 256), bf16),
        pltpu.VMEM((16, 16, 256), bf16),
        pltpu.VMEM((16, 16, 256), bf16),
        pltpu.VMEM((256, 256), jnp.float32),
        dma((5,)),
        dma((pieces,)), dma((count,)), dma((pieces,)),
        dma((count,)), dma((count,)), dma((count,)),
        dma((count * 3,)), dma((count * 9,)), dma((count * 3,)), dma((count * 6,)),
    ]
    for region in regions:
        w = region.width
        scratch += [
            pltpu.VMEM((2, 4, 256, w), bf16),
            pltpu.VMEM((6, 256, w), bf16),
            pltpu.VMEM((6, 64, w), bf16),
            pltpu.VMEM((6, 16, w), bf16),
            pltpu.VMEM((4, 256, w), bf16),
        ]

    anywhere = pl.BlockSpec(memory_space=pl.ANY)
    out = pl.pallas_call(
        lambda *refs: kernel(regions, half, *refs),
        out_shape=jax.ShapeDtypeStruct((batches * block, width), bf16),
        in_specs=[anywhere] * 4,
        out_specs=pl.BlockSpec(memory_space=pltpu.VMEM),
        scratch_shapes=scratch,
        name="ffn",
        compiler_params=pltpu.CompilerParams(
            collective_id=0, has_side_effects=True, vmem_limit_bytes=67_000_000
        ),
    )(tokens.reshape(batches * block, width), gate_weight, up_weight, down_weight)
    return out.reshape(batches, block, width)


def solution(mesh):
    spread = P(("row", "col"), None)
    return jax.shard_map(
        on_device,
        mesh=mesh,
        in_specs=(P(None, "col", "row"), spread, spread, spread),
        out_specs=P(None, "col", "row"),
        check_vma=False,
    )
```

time: 123 us -> 117 us (0.951)
  Pallas kernels: 121 us -> 115 us
    pallas_call x1, Pallas kernels: 121 us -> 115 us  [on_device(): pl.pallas_call(lambda *refs: kernel(regions, half, *refs), out_shape=jax....]
where the time goes in v2:
time: 117 us
  Pallas kernels  115 us (98%)
  local copies, waits for them, and re-layouts  1.47 us (1%)
    pallas_call x1, Pallas kernels, on_device(): pl.pallas_call(lambda *refs: kernel(regions, half, *refs), out_shape=jax....  115 us

profile of v2, /device:TPU:1, one launch (start us, length us, event | category | flops | bytes accessed | tf_op | source)
XLA Modules:
  0.0 116.9 jit_solution(14683202745445890403)
XLA Ops:
  0.0 115.4 %ffn.1 = bf16[16,2048]{1,0:T(8,128)(2,1)} custom-call(bf16[16,2048]{1,0:T(8,128)(2,1)} %bitcast.3, bf16[128,26624]{1,0:T(8,128)(2,1)} %refs_1_.1, bf16[128,26624]{1,0:T(8,128)(2,1)} %refs_2_.1, bf16[128,26624]{1,0:T(8,128)(2,1)} %refs_3_.1), custom_call_target="tpu_custom_call" | custom-call | tf_op jit(solution)/shard_map/ffn/pallas_call | solution.py:402
  115.4 1.5 %copy.6 = bf16[2,8,2048]{2,1,0:T(8,128)(2,1)} copy(bf16[2,8,2048]{2,1,0:T(8,128)(2,1)} %bitcast.2) | data formatting | bytes 131072

commit v3 on v2

--- a/solution.py
+++ b/solution.py
@@ -8,11 +8,16 @@
 MESH = pl.DeviceIdType.MESH
 SIDE = 4
 TILE = 128
-WAVES = ((3, 3, 3), (3, 3, 3), (3, 3, 2))
+WAVES = ((3, 2, 2), (2, 3, 2), (2, 2, 2), (2, 2, 2))
 GATE_OF = (1, 0, 0, 1, 0, 1)
 STEP_OF = (1, 1, -1, -1, 1, -1)
 LAG = 1
 ROWS = (256, 64, 16)
+
+
+def order_of(tasks):
+    waves = len(WAVES)
+    return [(wave, tick - LAG * wave) for tick in range(tasks + LAG * (waves - 1)) for wave in range(waves) if 0 <= tick - LAG * wave < tasks]
 
 
 class Region:
@@ -42,6 +47,7 @@
 def kernel(regions, half, *refs):
     tokens, gate_hbm, up_hbm, down_hbm, out = refs[:5]
     weights, gathered, parts, inbox, total = refs[5:10]
+    staged = refs[-1]
     exchange, w_own, w_send, w_recv, d_own, d_send, d_recv, red_send, red_recv, all_send, all_recv = refs[10:21]
     bufs = refs[21:]
     first = 0
@@ -63,7 +69,7 @@
     around = [[lax.rem(place[axis] + step, SIDE) for step in range(SIDE)] for axis in range(3)]
     near = {}
     for axis in range(3):
-        for step in (1, -1):
+        for step in (1, 2, -1):
             at = list(place)
             at[axis] = around[axis][step]
             near[axis, step] = device(*at)
@@ -124,7 +130,7 @@
     def token_copy(step):
         to = peers[step]
         return pltpu.make_async_remote_copy(
-            src_ref=tokens.at[:, pl.ds(multiple(lax.div(to, 2) * 256, 256), 256)],
+            src_ref=staged.at[lax.div(to, 2)],
             dst_ref=gathered.at[col],
             send_sem=exchange.at[0],
             recv_sem=exchange.at[1],
@@ -165,14 +171,27 @@
                 src_ref=sums_view(region, stage, GATE_OF[slot], step if slot < 4 else 2),
                 dst_ref=region.boxes[stage].at[slot],
                 send_sem=red_send.at[region.index * 3 + stage],
-                recv_sem=red_recv.at[(region.index * 3 + stage) * 3 + max(slot - 3, 0)],
+                recv_sem=red_recv.at[region.index * 7 + stage * 3 + max(slot - 3, 0)],
                 device_id=near[region.axes[stage], step],
                 device_id_type=MESH,
             ).start()
 
+    def send_last(region):
+        first = at_stage(region, 0)
+        for slot, step in enumerate((2, 1, -1)):
+            rows = pl.ds(rows_from(region, 2, step), ROWS[2])
+            pltpu.make_async_remote_copy(
+                src_ref=region.sums.at[:, first, rows],
+                dst_ref=region.box3.at[slot],
+                send_sem=red_send.at[region.index * 3 + 2],
+                recv_sem=red_recv.at[region.index * 7 + 6],
+                device_id=near[region.axes[2], step],
+                device_id_type=MESH,
+            ).start()
+
     def arrived(region, stage, group):
         box = region.boxes[stage]
-        drain(box.at[pl.ds(0, 4)] if group == 0 else box.at[group + 3], red_recv.at[(region.index * 3 + stage) * 3 + group])
+        drain(box.at[pl.ds(0, 4)] if group == 0 else box.at[group + 3], red_recv.at[region.index * 7 + stage * 3 + group])
 
     def add_rows(target, *terms):
         count = target.shape[0] // 16
@@ -224,7 +243,10 @@
             box = region.boxes[stage]
             add_rows(sums_view(region, stage, 0, 0), box.at[1], box.at[2])
             add_rows(sums_view(region, stage, 1, 0), box.at[0], box.at[3])
-            send_sums(region, stage + 1, 4, 5, 0, 2)
+            if stage == 0:
+                send_sums(region, 1, 4, 5, 0, 2)
+            else:
+                send_last(region)
 
         return run
 
@@ -241,13 +263,10 @@
             start = start + part * size
         return region.hidden.at[at, pl.ds(start if isinstance(start, int) else multiple(start, 16), size)]
 
-    def forwards(region, stage):
-        return (2, 3) if stage < 2 else (2 + (region.color + region.wave) % 2,)
-
     def send_hidden(region, stage, *slots):
         for slot in slots:
             step = 1 if slot % 2 == 0 else -1
-            view = hidden_view(region, stage, 0 if slot < 2 else -step, slot - 2 if slot >= 2 and stage < 2 else None)
+            view = hidden_view(region, stage, 0 if slot < 2 else -step, slot - 2 if slot >= 2 else None)
             pltpu.make_async_remote_copy(
                 src_ref=view,
                 dst_ref=view,
@@ -257,6 +276,18 @@
                 device_id_type=MESH,
             ).start()
 
+    def send_first(region):
+        view = hidden_view(region, 2, 0)
+        for step in (2, 1, -1):
+            pltpu.make_async_remote_copy(
+                src_ref=view,
+                dst_ref=view,
+                send_sem=all_send.at[region.index * 3 + 2],
+                recv_sem=all_recv.at[(region.index * 3 + 2) * 2],
+                device_id=near[region.axes[2], step],
+                device_id_type=MESH,
+            ).start()
+
     def hidden_rows(region, stage, count):
         if stage == 0 and count > 1:
             return region.hidden.at[pl.ds(0, count)]
@@ -266,25 +297,32 @@
         drain(hidden_rows(region, stage, 2 - group), all_recv.at[(region.index * 3 + stage) * 2 + group])
 
     def task_hidden(region):
-        arrived(region, 2, 0)
         box = region.box3
-        gate = sums_view(region, 2, 0, 0)[...].astype(jnp.float32)
-        gate = gate + box[1].astype(jnp.float32) + box[2].astype(jnp.float32)
-        up = sums_view(region, 2, 1, 0)[...].astype(jnp.float32)
-        up = up + box[0].astype(jnp.float32) + box[3].astype(jnp.float32)
+        drain(box, red_recv.at[region.index * 7 + 6])
+        at, rows = at_stage(region, 0), pl.ds(rows_from(region, 2, 0), ROWS[2])
+        gate, up = (
+            region.sums[matrix, at, rows].astype(jnp.float32)
+            + box[0, matrix].astype(jnp.float32)
+            + box[1, matrix].astype(jnp.float32)
+            + box[2, matrix].astype(jnp.float32)
+            for matrix in range(2)
+        )
         hidden_view(region, 2, 0)[...] = (gate / (1.0 + jnp.exp(-gate)) * up).astype(jnp.bfloat16)
-        send_hidden(region, 2, 0, 1)
+        send_first(region)
 
     def task_forward(stage):
         def run(region):
             reached(region, stage, 0)
-            send_hidden(region, stage, *forwards(region, stage))
+            send_hidden(region, stage, 2, 3)
 
         return run
 
     def task_gathered(stage):
         def run(region):
-            reached(region, stage, 1)
+            if stage == 2:
+                drain(hidden_rows(region, 2, 3), all_recv.at[(region.index * 3 + 2) * 2])
+            else:
+                reached(region, stage, 1)
             send_hidden(region, stage - 1, 0, 1)
 
         return run
@@ -304,25 +342,24 @@
             project(region, quarter)
 
     tasks = (
-        task_first, task_second, task_relay(0), task_settle(0), task_relay(1), task_settle(1), task_relay(2),
-        task_hidden, task_forward(2), task_gathered(2), task_forward(1), task_gathered(1), task_forward(0), task_project,
+        task_first, task_second, task_relay(0), task_settle(0), task_relay(1), task_settle(1),
+        task_hidden, task_gathered(2), task_forward(1), task_gathered(1), task_forward(0), task_project,
     )
 
+    for block in range(cols // 2):
+        pltpu.make_async_copy(tokens.at[:, pl.ds(block * 256, 256)], staged.at[block], exchange.at[4]).start()
     for region, position in weight_order():
         for matrix in range(2):
             term_weight(region, matrix, position, False).start()
-    own_tokens = pltpu.make_async_copy(
-        tokens.at[:, pl.ds(multiple(chip * 256, 256), 256)], gathered.at[col], exchange.at[4]
-    )
-    own_tokens.start()
+    drain(staged, exchange.at[4])
 
     barrier = pltpu.get_barrier_semaphore()
     for step in range(1, cols):
         pl.semaphore_signal(barrier, inc=1, device_id=(row, peers[step]), device_id_type=MESH)
     for axis in (1, 2):
-        for step in (1, -1):
+        for step in (1, 2, -1):
             pl.semaphore_signal(barrier, inc=1, device_id=near[axis, step], device_id_type=MESH)
-    pl.semaphore_wait(barrier, cols - 1 + 4)
+    pl.semaphore_wait(barrier, cols - 1 + 6)
 
     for step in range(1, cols):
         token_copy(step).start()
@@ -334,17 +371,13 @@
         down_weight(region, True).start()
 
     total[...] = jnp.zeros_like(total)
-    own_tokens.wait()
+    gathered[col] = staged[chip]
     drain(gathered.at[others], exchange.at[1])
 
-    waves = len(WAVES)
-    for tick in range(len(tasks) + LAG * (waves - 1)):
-        for wave in range(waves):
-            number = tick - LAG * wave
-            if 0 <= number < len(tasks):
-                for region in regions:
-                    if region.wave == wave:
-                        tasks[number](region)
+    for wave, number in order_of(len(tasks)):
+        for region in regions:
+            if region.wave == wave:
+                tasks[number](region)
 
     parts[...] = total[...].astype(jnp.bfloat16).reshape(cols, 16, 256)
     for step in range(1, cols):
@@ -386,7 +419,7 @@
         dma((5,)),
         dma((pieces,)), dma((count,)), dma((pieces,)),
         dma((count,)), dma((count,)), dma((count,)),
-        dma((count * 3,)), dma((count * 9,)), dma((count * 3,)), dma((count * 6,)),
+        dma((count * 3,)), dma((count * 7,)), dma((count * 3,)), dma((count * 6,)),
     ]
     for region in regions:
         w = region.width
@@ -394,10 +427,11 @@
             pltpu.VMEM((2, 4, 256, w), bf16),
             pltpu.VMEM((6, 256, w), bf16),
             pltpu.VMEM((6, 64, w), bf16),
-            pltpu.VMEM((6, 16, w), bf16),
+            pltpu.VMEM((3, 2, 16, w), bf16),
             pltpu.VMEM((4, 256, w), bf16),
         ]
 
+    scratch.append(pltpu.VMEM((8, 16, 256), bf16))
     anywhere = pl.BlockSpec(memory_space=pl.ANY)
     out = pl.pallas_call(
         lambda *refs: kernel(regions, half, *refs),

time: 117 us -> 112 us (0.957)
  Pallas kernels: 115 us -> 111 us
    pallas_call x1, Pallas kernels: 115 us -> 111 us  [on_device(): pl.pallas_call(lambda *refs: kernel(regions, half, *refs), out_shape=jax....]
where the time goes in v3:
time: 112 us
  Pallas kernels  111 us (99%)
  local copies, waits for them, and re-layouts  1.47 us (1%)
    pallas_call x1, Pallas kernels, on_device(): pl.pallas_call(lambda *refs: kernel(regions, half, *refs), out_shape=jax....  111 us

profile of v3, /device:TPU:1, one launch (start us, length us, event | category | flops | bytes accessed | tf_op | source)
XLA Modules:
  0.0 112.1 jit_solution(15105215892690694708)
XLA Ops:
  0.0 110.7 %ffn.1 = bf16[16,2048]{1,0:T(8,128)(2,1)} custom-call(bf16[16,2048]{1,0:T(8,128)(2,1)} %bitcast.3, bf16[128,26624]{1,0:T(8,128)(2,1)} %refs_1_.1, bf16[128,26624]{1,0:T(8,128)(2,1)} %refs_2_.1, bf16[128,26624]{1,0:T(8,128)(2,1)} %refs_3_.1), custom_call_target="tpu_custom_call" | custom-call | tf_op jit(solution)/shard_map/ffn/pallas_call | solution.py:436
  110.7 1.5 %copy.6 = bf16[2,8,2048]{2,1,0:T(8,128)(2,1)} copy(bf16[2,8,2048]{2,1,0:T(8,128)(2,1)} %bitcast.2) | data formatting | bytes 131072

commit v4 on v3

--- a/solution.py
+++ b/solution.py
@@ -8,16 +8,20 @@
 MESH = pl.DeviceIdType.MESH
 SIDE = 4
 TILE = 128
-WAVES = ((3, 2, 2), (2, 3, 2), (2, 2, 2), (2, 2, 2))
+WAVES = ((1, 1, 1), (2, 2, 2), (2, 2, 2), (2, 2, 2), (2, 2, 1))
 GATE_OF = (1, 0, 0, 1, 0, 1)
 STEP_OF = (1, 1, -1, -1, 1, -1)
-LAG = 1
+ORDER = (0, 0, 1, 1, 0, 4, 2, 0, 1, 3, 2, 0, 1, 2, 3, 0, 1, 3, 2, 1, 4, 0, 2, 3, 4, 3, 0, 1, 2, 4, 0, 3, 1, 2, 4, 0, 1, 3, 4, 2, 1, 4, 3, 2, 0, 1, 3, 4, 2, 4, 3, 4, 3, 2, 0, 1, 4, 3, 2, 4)
 ROWS = (256, 64, 16)
 
 
 def order_of(tasks):
-    waves = len(WAVES)
-    return [(wave, tick - LAG * wave) for tick in range(tasks + LAG * (waves - 1)) for wave in range(waves) if 0 <= tick - LAG * wave < tasks]
+    done, order = [0] * len(WAVES), []
+    for wave in ORDER:
+        order.append((wave, done[wave]))
+        done[wave] += 1
+    assert all(count == tasks for count in done)
+    return order
 
 
 class Region:
@@ -314,6 +318,12 @@
         def run(region):
             reached(region, stage, 0)
             send_hidden(region, stage, 2, 3)
+            if stage == 0:
+                columns = pl.ds(region.offset, SIDE * region.width)
+                drain(weights.at[2, pl.ds(0, TILE), columns], d_own.at[region.index])
+                drain(weights.at[2, pl.ds(0, TILE), columns], d_recv.at[region.index])
+                for step in (0, 1, -1):
+                    project(region, at_stage(region, 0, step))
 
         return run
 
@@ -334,12 +344,8 @@
         )
 
     def task_project(region):
-        drain(weights.at[2, pl.ds(0, TILE), pl.ds(region.offset, SIDE * region.width)], d_own.at[region.index])
-        drain(weights.at[2, pl.ds(0, TILE), pl.ds(region.offset, SIDE * region.width)], d_recv.at[region.index])
         reached(region, 0, 1)
-
-        for quarter in range(SIDE):
-            project(region, quarter)
+        project(region, at_stage(region, 0, 2))
 
     tasks = (
         task_first, task_second, task_relay(0), task_settle(0), task_relay(1), task_settle(1),

time: 112 us -> 108 us (0.964)
  Pallas kernels: 111 us -> 107 us
    pallas_call x1, Pallas kernels: 111 us -> 107 us  [on_device(): pl.pallas_call(lambda *refs: kernel(regions, half, *refs), out_shape=jax....]
where the time goes in v4:
time: 108 us
  Pallas kernels  107 us (99%)
  local copies, waits for them, and re-layouts  1.47 us (1%)
    pallas_call x1, Pallas kernels, on_device(): pl.pallas_call(lambda *refs: kernel(regions, half, *refs), out_shape=jax....  107 us

profile of v4, /device:TPU:1, one launch (start us, length us, event | category | flops | bytes accessed | tf_op | source)
XLA Modules:
  0.0 108.3 jit_solution(2480882505511753632)
XLA Ops:
  0.0 106.8 %ffn.1 = bf16[16,2048]{1,0:T(8,128)(2,1)} custom-call(bf16[16,2048]{1,0:T(8,128)(2,1)} %bitcast.3, bf16[128,26624]{1,0:T(8,128)(2,1)} %refs_1_.1, bf16[128,26624]{1,0:T(8,128)(2,1)} %refs_2_.1, bf16[128,26624]{1,0:T(8,128)(2,1)} %refs_3_.1), custom_call_target="tpu_custom_call" | custom-call | tf_op jit(solution)/shard_map/ffn/pallas_call | solution.py:442
  106.8 1.5 %copy.6 = bf16[2,8,2048]{2,1,0:T(8,128)(2,1)} copy(bf16[2,8,2048]{2,1,0:T(8,128)(2,1)} %bitcast.2) | data formatting | bytes 131072

commit v5 on v4

--- a/solution.py
+++ b/solution.py
@@ -52,8 +52,8 @@
     tokens, gate_hbm, up_hbm, down_hbm, out = refs[:5]
     weights, gathered, parts, inbox, total = refs[5:10]
     staged = refs[-1]
-    exchange, w_own, w_send, w_recv, d_own, d_send, d_recv, red_send, red_recv, all_send, all_recv = refs[10:21]
-    bufs = refs[21:]
+    exchange, shared, w_own, w_recv, red_recv, all_recv = refs[10:16]
+    bufs = refs[16:]
     first = 0
     for index, region in enumerate(regions):
         region.index, region.first = index, first
@@ -109,7 +109,7 @@
     def term_weight(region, matrix, position, remote):
         quarter = quarters(region)[position] if region.wave == 0 else None
         index = region.first + position
-        sems = (w_own.at[index], w_send.at[region.index], w_recv.at[index])
+        sems = (w_own.at[index], shared.at[0], w_recv.at[index])
         return weight_copy(region, matrix, quarter, sems, remote)
 
     def wait_weights(region, position):
@@ -119,8 +119,7 @@
         drain(both, w_recv.at[region.first + position])
 
     def down_weight(region, remote):
-        index = region.index
-        return weight_copy(region, 2, None, (d_own.at[index], d_send.at[index], d_recv.at[index]), remote)
+        return weight_copy(region, 2, None, (shared.at[1], shared.at[2], shared.at[3]), remote)
 
     def weight_order():
         for position in range(4):
@@ -174,7 +173,7 @@
             pltpu.make_async_remote_copy(
                 src_ref=sums_view(region, stage, GATE_OF[slot], step if slot < 4 else 2),
                 dst_ref=region.boxes[stage].at[slot],
-                send_sem=red_send.at[region.index * 3 + stage],
+                send_sem=shared.at[4 + stage],
                 recv_sem=red_recv.at[region.index * 7 + stage * 3 + max(slot - 3, 0)],
                 device_id=near[region.axes[stage], step],
                 device_id_type=MESH,
@@ -187,7 +186,7 @@
             pltpu.make_async_remote_copy(
                 src_ref=region.sums.at[:, first, rows],
                 dst_ref=region.box3.at[slot],
-                send_sem=red_send.at[region.index * 3 + 2],
+                send_sem=shared.at[6],
                 recv_sem=red_recv.at[region.index * 7 + 6],
                 device_id=near[region.axes[2], step],
                 device_id_type=MESH,
@@ -274,7 +273,7 @@
             pltpu.make_async_remote_copy(
                 src_ref=view,
                 dst_ref=view,
-                send_sem=all_send.at[region.index * 3 + stage],
+                send_sem=shared.at[7 + stage],
                 recv_sem=all_recv.at[(region.index * 3 + stage) * 2 + slot // 2],
                 device_id=near[region.axes[stage], step],
                 device_id_type=MESH,
@@ -286,7 +285,7 @@
             pltpu.make_async_remote_copy(
                 src_ref=view,
                 dst_ref=view,
-                send_sem=all_send.at[region.index * 3 + 2],
+                send_sem=shared.at[9],
                 recv_sem=all_recv.at[(region.index * 3 + 2) * 2],
                 device_id=near[region.axes[2], step],
                 device_id_type=MESH,
@@ -319,9 +318,6 @@
             reached(region, stage, 0)
             send_hidden(region, stage, 2, 3)
             if stage == 0:
-                columns = pl.ds(region.offset, SIDE * region.width)
-                drain(weights.at[2, pl.ds(0, TILE), columns], d_own.at[region.index])
-                drain(weights.at[2, pl.ds(0, TILE), columns], d_recv.at[region.index])
                 for step in (0, 1, -1):
                     project(region, at_stage(region, 0, step))
 
@@ -347,9 +343,10 @@
         reached(region, 0, 1)
         project(region, at_stage(region, 0, 2))
 
+    first_product = task_forward(0)
     tasks = (
         task_first, task_second, task_relay(0), task_settle(0), task_relay(1), task_settle(1),
-        task_hidden, task_gathered(2), task_forward(1), task_gathered(1), task_forward(0), task_project,
+        task_hidden, task_gathered(2), task_forward(1), task_gathered(1), first_product, task_project,
     )
 
     for block in range(cols // 2):
@@ -380,7 +377,12 @@
     gathered[col] = staged[chip]
     drain(gathered.at[others], exchange.at[1])
 
+    down_waited = False
     for wave, number in order_of(len(tasks)):
+        if tasks[number] is first_product and not down_waited:
+            down_waited = True
+            for sem in (1, 3):
+                drain(weights.at[2, pl.ds(0, TILE)], shared.at[sem])
         for region in regions:
             if region.wave == wave:
                 tasks[number](region)
@@ -397,13 +399,14 @@
 
     drain(gathered.at[others], exchange.at[0])
     drain(parts.at[others], exchange.at[2])
-    for region in regions:
-        columns = pl.ds(region.offset, SIDE * region.width)
-        drain(weights.at[pl.ds(0, 2), pl.ds(0, TILE), columns], w_send.at[region.index])
-        drain(weights.at[2, pl.ds(0, TILE), columns], d_send.at[region.index])
-        for stage in range(3):
-            drain(region.boxes[stage], red_send.at[region.index * 3 + stage])
-            drain(hidden_rows(region, stage, 3), all_send.at[region.index * 3 + stage])
+    drain(weights.at[pl.ds(0, 2), pl.ds(0, TILE)], shared.at[0])
+    drain(weights.at[2, pl.ds(0, TILE)], shared.at[2])
+    drain(weights.at[:, pl.ds(0, 128)], shared.at[4])
+    drain(weights.at[:, pl.ds(0, 32)], shared.at[5])
+    drain(weights.at[:, pl.ds(0, 16), pl.ds(0, half // 2)], shared.at[6])
+    drain(weights.at[0, pl.ds(0, 192)], shared.at[7])
+    drain(weights.at[0, pl.ds(0, 48)], shared.at[8])
+    drain(weights.at[0, pl.ds(0, 48), pl.ds(0, half // 4)], shared.at[9])
 
 
 def on_device(tokens, gate_weight, up_weight, down_weight):
@@ -422,10 +425,7 @@
         pltpu.VMEM((16, 16, 256), bf16),
         pltpu.VMEM((16, 16, 256), bf16),
         pltpu.VMEM((256, 256), jnp.float32),
-        dma((5,)),
-        dma((pieces,)), dma((count,)), dma((pieces,)),
-        dma((count,)), dma((count,)), dma((count,)),
-        dma((count * 3,)), dma((count * 7,)), dma((count * 3,)), dma((count * 6,)),
+        dma((5,)), dma((10,)), dma((pieces,)), dma((pieces,)), dma((count * 7,)), dma((count * 6,)),
     ]
     for region in regions:
         w = region.width

time: 108 us -> 107 us (level)
  Pallas kernels: 107 us -> 105 us
    pallas_call x1, Pallas kernels: 107 us -> 105 us  [on_device(): pl.pallas_call(lambda *refs: kernel(regions, half, *refs), out_shape=jax....]
where the time goes in v5:
time: 107 us
  Pallas kernels  105 us (98%)
  local copies, waits for them, and re-layouts  1.47 us (1%)
    pallas_call x1, Pallas kernels, on_device(): pl.pallas_call(lambda *refs: kernel(regions, half, *refs), out_shape=jax....  105 us

profile of v5, /device:TPU:1, one launch (start us, length us, event | category | flops | bytes accessed | tf_op | source)
XLA Modules:
  0.0 106.8 jit_solution(600295260073647350)
XLA Ops:
  0.0 105.3 %ffn.1 = bf16[16,2048]{1,0:T(8,128)(2,1)} custom-call(bf16[16,2048]{1,0:T(8,128)(2,1)} %bitcast.3, bf16[128,26624]{1,0:T(8,128)(2,1)} %refs_1_.1, bf16[128,26624]{1,0:T(8,128)(2,1)} %refs_2_.1, bf16[128,26624]{1,0:T(8,128)(2,1)} %refs_3_.1), custom_call_target="tpu_custom_call" | custom-call | tf_op jit(solution)/shard_map/ffn/pallas_call | solution.py:442
  105.3 1.5 %copy.6 = bf16[2,8,2048]{2,1,0:T(8,128)(2,1)} copy(bf16[2,8,2048]{2,1,0:T(8,128)(2,1)} %bitcast.2) | data formatting | bytes 131072
